TPU v7x, 32 devices: a whole 2x2x4 slice. The times are simulated.
32 devices in a mesh: row: 8 (over y, x, core), col: 4 (over z).
Axes of the slice: x: 2, y: 2, z: 4, core: 2. Of those that a mesh axis runs over, the one named last changes fastest.
Arguments:
- iterate_t: bfloat16 [8, 4, 1024, 32768], P(None, 'col', None, 'row'), may hold values from -0.03125 to 0.03125
- vectors: bfloat16 [32768, 256], P(('row', 'col')), may hold values from -6 to 6
- old_factor_t: bfloat16 [512, 32768], P('col', 'row'), may hold values from -5 to 5
Outputs:
- panel: float32 [32768, 256], P(('row', 'col'))
- basis: float32 [768, 32768], P('col', 'row')
All inputs are finite; a program needn't handle non-finite values.
Results may differ from a plain program's by a relative error of at most 0.0013.
Values may be sent and summed in bfloat16 or wider, within the bound.
No kernel may reach another device: no remote copies, remote signals or barrier semaphores. Data moves between devices by JAX's collectives and lax.ppermute only.
A program may use at most 192 MiB of HBM per device.

v0:
```python
import jax
import jax.numpy as jnp
from jax import lax
from jax.sharding import PartitionSpec as P

NSTATE = 32768


def body(iterate_t, vectors, old_factor_t):
    flat_iterate = iterate_t.reshape(-1, iterate_t.shape[-1])
    highest = lax.Precision.HIGHEST

    def apply_iterate(vector):
        gathered = lax.all_gather(vector, "row", axis=0, tiled=True)
        return lax.psum_scatter(
            lax.dot_general(
                flat_iterate, gathered, (((0,), (0,)), ((), ())), preferred_element_type=jnp.float32
            ),
            "col",
            scatter_dimension=0,
            tiled=True,
        )

    first_full = apply_iterate(vectors)
    second = apply_iterate(first_full.astype(jnp.bfloat16)).astype(jnp.bfloat16)
    panel = 1.5 * first_full - 0.5 * apply_iterate(second)
    old_gathered = lax.all_gather(old_factor_t, "col", axis=0, tiled=True)
    panel_gathered = lax.all_gather(panel, "col", axis=0, tiled=True)
    old_full = old_gathered.astype(jnp.float32)
    scale_gram = 1.0 / NSTATE
    column = lax.axis_index("col")
    groups = lax.axis_size("col")
    old_old = lax.dot_general(
        old_gathered, old_gathered, (((1,), (1,)), ((), ())), preferred_element_type=jnp.float32
    )
    old_panel = jnp.dot(old_full, panel_gathered, precision=highest)
    panel_panel = lax.dot_general(
        panel_gathered, panel_gathered, (((0,), (0,)), ((), ())), precision=highest
    )
    local_gram = (
        jnp.concatenate(
            [
                jnp.concatenate([old_old, old_panel], 1),
                jnp.concatenate([old_panel.T, panel_panel], 1),
            ],
            0,
        )
        * scale_gram
    )
    gram = lax.psum(local_gram, "row")
    lower_factor = jnp.linalg.cholesky(gram)
    identity = jnp.eye(gram.shape[0], dtype=jnp.float32)
    inverse = jax.scipy.linalg.solve_triangular(lower_factor, identity, lower=True)
    basis_share = gram.shape[0] // groups
    inverse_rows = lax.dynamic_slice_in_dim(inverse, column * basis_share, basis_share, 0)
    old_count = old_gathered.shape[0]
    basis = jnp.dot(inverse_rows[:, :old_count], old_full, precision=highest)
    basis = basis + lax.dot_general(
        inverse_rows[:, old_count:], panel_gathered, (((1,), (1,)), ((), ())), precision=highest
    )
    return (panel, basis)


def solution(mesh):
    return jax.shard_map(
        body,
        mesh=mesh,
        in_specs=(P(None, "col", None, "row"), P(("row", "col"), None), P("col", "row")),
        out_specs=(P(("row", "col"), None), P("col", "row")),
        check_vma=False,
    )
```

profile of v0, /device:TPU:0, one launch (start us, length us, event | category | flops | bytes accessed | tf_op | source)
XLA Modules:
  0.0 959.2 jit_solution(827991322288170241)
XLA Ops:
  7.2 0.7 all-gather.6.cloned.1.call-update
  7.9 41.3 %all-gather.6.cloned.1.call-done = bf16[8192,256]{1,0:T(8,128)(2,1)} async-done(((bf16[1024,256]{1,0:T(8,128)(2,1)}), bf16[8192,256]{1,0:T(8,128)(2,1)}) %all-gather.6.cloned.1.call-update) | async-done | bytes 4194320 | tf_op jit(solution)/shard_map/all_gather | solution.py:14
  49.2 30.1 %fusion.59 = f32[4096,256]{1,0:T(8,128)} fusion(bf16[8192,4096]{1,0:T(8,128)(2,1)} %bitcast, bf16[8192,256]{1,0:T(8,128)(2,1)} %all-gather.6.cloned.1.call-done), kind=kOutput, calls=%fused_computation.124 | convolution fusion | flops 17179869184 | bytes 75497472 | tf_op jit(solution)/shard_map/dot_general | solution.py:16
  79.4 76.9 %reduce-scatter.4.cloned.1.call-done = f32[1024,256]{1,0:T(8,128)} async-done(((f32[4096,256]{1,0:T(8,128)}), f32[1024,256]{1,0:T(8,128)}) %reduce-scatter.4.cloned.1.call-update) | async-done | bytes 1048592 | tf_op jit(solution)/shard_map/reduce_scatter | solution.py:15
  156.3 2.1 convert_element_type.18
  158.6 37.2 %all-gather.8.cloned.1.call-done = bf16[8192,256]{1,0:T(8,128)(2,1)} async-done(((bf16[1024,256]{1,0:T(8,128)(2,1)}), bf16[8192,256]{1,0:T(8,128)(2,1)}) %all-gather.8.cloned.1.call-update) | async-done | bytes 4194320 | tf_op jit(solution)/shard_map/all_gather | solution.py:14
  195.9 30.1 %convolution_bitcast_fusion.1 = f32[4096,256]{0,1:T(8,128)} fusion(bf16[8192,256]{1,0:T(8,128)(2,1)} %all-gather.8.cloned.1.call-done, bf16[8192,4096]{1,0:T(8,128)(2,1)} %bitcast), kind=kOutput, calls=%fused_computation.3 | convolution fusion | flops 17179869184 | bytes 75497472 | tf_op jit(solution)/shard_map/dot_general | solution.py:16
  226.0 76.9 %reduce-scatter.6.cloned.1.call-done = f32[1024,256]{0,1:T(8,128)} async-done(((f32[4096,256]{0,1:T(8,128)}), f32[1024,256]{0,1:T(8,128)}) %reduce-scatter.6.cloned.1.call-update) | async-done | bytes 1048592 | tf_op jit(solution)/shard_map/reduce_scatter | solution.py:15
  302.9 2.1 convert_element_type.19
  305.1 37.3 %all-gather.10.cloned.1.call-done = bf16[8192,256]{0,1:T(8,128)(2,1)} async-done(((bf16[1024,256]{0,1:T(8,128)(2,1)}), bf16[8192,256]{0,1:T(8,128)(2,1)}) %all-gather.10.cloned.1.call-update) | async-done | bytes 4194320 | tf_op jit(solution)/shard_map/all_gather | solution.py:14
  342.4 35.5 %convolution_bitcast_fusion = f32[4096,256]{1,0:T(8,128)} fusion(bf16[8192,256]{0,1:T(8,128)(2,1)} %all-gather.10.cloned.1.call-done, bf16[8192,4096]{1,0:T(8,128)(2,1)} %bitcast), kind=kOutput, calls=%fused_computation.2 | convolution fusion | flops 17179869184 | bytes 75497472 | tf_op jit(solution)/shard_map/dot_general | solution.py:16
  377.9 0.7 all-gather.12.cloned.1.call-update
  379.1 75.7 %reduce-scatter.8.cloned.1.call-done = f32[1024,256]{1,0:T(8,128)} async-done(((f32[4096,256]{1,0:T(8,128)}), f32[1024,256]{1,0:T(8,128)}) %reduce-scatter.8.cloned.1.call-update) | async-done | bytes 1048592 | tf_op jit(solution)/shard_map/reduce_scatter | solution.py:15
  454.8 2.3 multiply_subtract_fusion
  457.2 80.5 %all-gather.12.cloned.1.call-done = bf16[512,4096]{1,0:T(8,128)(2,1)} async-done(((bf16[128,4096]{1,0:T(8,128)(2,1)}), bf16[512,4096]{1,0:T(8,128)(2,1)}) %all-gather.12.cloned.1.call-update) | async-done | bytes 4194320 | tf_op jit(solution)/shard_map/all_gather | solution.py:27
  537.7 5.8 fusion.60
  543.5 75.6 %all-gather.14.cloned.1.call-done = f32[4096,256]{1,0:T(8,128)} async-done(((f32[1024,256]{1,0:T(8,128)}), f32[4096,256]{1,0:T(8,128)}) %all-gather.14.cloned.1.call-update) | async-done | bytes 4194320 | tf_op jit(solution)/shard_map/all_gather | solution.py:28
  619.1 9.8 %fusion.61 = f32[256,512]{1,0:T(8,128)S(1)} fusion(f32[4096,256]{1,0:T(8,128)} %all-gather.14.cloned.1.call-done, bf16[512,4096]{1,0:T(8,128)(2,1)} %all-gather.12.cloned.1.call-done), kind=kOutput, calls=%fused_computation.126 | convolution fusion | flops 6442450944 | bytes 8912896 | tf_op jit(solution)/shard_map/dot_general | solution.py:36
  629.1 10.2 %fusion.62 = f32[256,256]{0,1:T(8,128)S(1)} fusion(f32[4096,256]{1,0:T(8,128)} %all-gather.14.cloned.1.call-done), kind=kOutput, calls=%fused_computation.127 | convolution fusion | flops 3221225472 | bytes 4456448 | tf_op jit(solution)/shard_map/dot_general | solution.py:37
  639.4 1.6 maximum_multiply_fusion
  641.2 1.6 fusion.20
  642.8 59.8 %all-reduce.3.cloned.1.call-done = f32[768,768]{0,1:T(8,128)} async-done(((f32[768,768]{0,1:T(8,128)}), f32[768,768]{0,1:T(8,128)}) %all-reduce.3.cloned.1.call-update) | async-done | bytes 2359312 | tf_op jit(solution)/shard_map/psum | solution.py:50
  702.6 3.3 copy.7
  706.0 2.0 fusion
  708.0 1.4 copy-done.4
  709.4 11.7 %cholesky.165 = f32[128,128]{1,0:T(8,128)S(1)} custom-call(f32[128,128]{1,0:T(8,128)S(1)} %cholesky.424), custom_call_target="Cholesky" | custom-call | tf_op jit(solution)/shard_map/jit(cholesky)/cholesky | solution.py:51
  721.1 9.8 %custom-call.47 = f32[1,128,128]{1,2,0:T(8,128)S(1)} custom-call(f32[1,128,128]{2,1,0:T(8,128)S(1)} %get-tuple-element.45), custom_call_target="InvertDiagBlocksLowerTriangular" | custom-call | tf_op jit(solution)/shard_map/jit(cholesky)/cholesky | solution.py:51
  731.1 1.4 constant_dynamic-update-slice_fusion.15
  732.5 1.4 convolution_subtract_fusion.4
  733.9 11.7 %cholesky.188 = f32[128,128]{1,0:T(8,128)S(1)} custom-call(f32[128,128]{1,0:T(8,128)S(1)} %cholesky.428), custom_call_target="Cholesky" | custom-call | tf_op jit(solution)/shard_map/jit(cholesky)/cholesky | solution.py:51
  745.7 10.2 %custom-call.48 = f32[1,128,128]{1,2,0:T(8,128)S(1)} custom-call(f32[1,128,128]{2,1,0:T(8,128)S(1)} %get-tuple-element.42), custom_call_target="InvertDiagBlocksLowerTriangular" | custom-call | tf_op jit(solution)/shard_map/jit(cholesky)/cholesky | solution.py:51
  756.2 1.5 convolution_subtract_fusion.5
  757.8 11.7 %cholesky.354 = f32[128,128]{1,0:T(8,128)S(1)} custom-call(f32[128,128]{1,0:T(8,128)S(1)} %cholesky.433), custom_call_target="Cholesky" | custom-call | tf_op jit(solution)/shard_map/jit(cholesky)/cholesky | solution.py:51
  769.5 0.7 compare_reduce_fusion.3
  770.2 9.8 %custom-call.49 = f32[1,128,128]{1,2,0:T(8,128)S(1)} custom-call(f32[1,128,128]{2,1,0:T(8,128)S(1)} %get-tuple-element.39), custom_call_target="InvertDiagBlocksLowerTriangular" | custom-call | tf_op jit(solution)/shard_map/jit(cholesky)/cholesky | solution.py:51
  780.3 1.6 convolution_subtract_fusion.6
  781.9 11.9 %cholesky.373 = f32[128,128]{1,0:T(8,128)S(1)} custom-call(f32[128,128]{1,0:T(8,128)S(1)} %cholesky.438), custom_call_target="Cholesky" | custom-call | tf_op jit(solution)/shard_map/jit(cholesky)/cholesky | solution.py:51
  793.8 0.7 compare_reduce_fusion.2
  794.5 9.8 %custom-call.50 = f32[1,128,128]{1,2,0:T(8,128)S(1)} custom-call(f32[1,128,128]{2,1,0:T(8,128)S(1)} %get-tuple-element.36), custom_call_target="InvertDiagBlocksLowerTriangular" | custom-call | tf_op jit(solution)/shard_map/jit(cholesky)/cholesky | solution.py:51
  804.6 1.5 convolution_subtract_fusion.7
  806.1 11.7 %cholesky.392 = f32[128,128]{1,0:T(8,128)S(1)} custom-call(f32[128,128]{1,0:T(8,128)S(1)} %cholesky.443), custom_call_target="Cholesky" | custom-call | tf_op jit(solution)/shard_map/jit(cholesky)/cholesky | solution.py:51
  817.9 0.6 compare_reduce_fusion.1
  818.5 9.8 %custom-call.51 = f32[1,128,128]{1,2,0:T(8,128)S(1)} custom-call(f32[1,128,128]{2,1,0:T(8,128)S(1)} %get-tuple-element.33), custom_call_target="InvertDiagBlocksLowerTriangular" | custom-call | tf_op jit(solution)/shard_map/jit(cholesky)/cholesky | solution.py:51
  828.5 1.3 convolution_subtract_fusion.8
  829.8 11.7 %cholesky.410 = f32[128,128]{1,0:T(8,128)S(1)} custom-call(f32[128,128]{1,0:T(8,128)S(1)} %convolution_subtract_fusion.8), custom_call_target="Cholesky" | custom-call | tf_op jit(solution)/shard_map/jit(cholesky)/cholesky | solution.py:51
  841.6 0.7 compare_reduce_fusion
  842.2 0.7 compare_reduce_fusion.4
  846.8 1.6 select_select_fusion
  848.3 21.1 %while.1 = (s32[]{:T(128)}, f32[768,768]{1,0:T(8,128)}, s32[6,2]{0,1:T(2,128)S(1)}, f32[6,128,128]{2,1,0:T(8,128)}, s32[]{:T(128)}) while((s32[]{:T(128)}, f32[768,768]{1,0:T(8,128)}, s32[6,2]{0,1:T(2,128)S(1)}, f32[6,128,128]{2,1,0:T(8,128)}, s32[]{:T(128)}) %tuple.44), condition=%wide.while_cond, body=%wide.while_body.sunk | while | flops 2 | bytes 132705 | solution.py:53
  849.0 2.9 bitcast_dynamic-update-slice_fusion.2
  852.6 2.9 bitcast_dynamic-update-slice_fusion.2
  856.1 2.9 bitcast_dynamic-update-slice_fusion.2
  859.6 2.9 bitcast_dynamic-update-slice_fusion.2
  863.1 2.9 bitcast_dynamic-update-slice_fusion.2
  866.6 2.8 bitcast_dynamic-update-slice_fusion.2
  869.4 60.6 %custom-call.52 = f32[6,128,128]{1,2,0:T(8,128)} custom-call(f32[6,128,128]{2,1,0:T(8,128)} %get-tuple-element.9), custom_call_target="InvertDiagBlocksLowerTriangular" | custom-call | tf_op jit(solution)/shard_map/jit(_solve_triangular)/triangular_solve | solution.py:53
  930.0 1.3 constant_dynamic-update-slice_fusion.4
  931.3 1.5 convolution_subtract_fusion.2
  933.4 1.5 convolution_subtract_fusion.3
  935.4 1.8 convolution_subtract_fusion.1
  937.8 2.0 fusion.9
  940.3 2.6 convolution_subtract_fusion
  943.4 2.8 fusion.24
  946.2 6.2 convolution_add_fusion
  (67 shorter events, 9.5 us)
Async XLA Ops:
  7.2 42.0 %all-gather.6.cloned.1.call-start = ((), (), s32[]{:S(2)}) async-start(), calls=%async_computation.3 | async-start | bytes 4718592 | tf_op jit(solution)/shard_map/all_gather | solution.py:14
  7.9 148.4 %reduce-scatter.4.cloned.1.call-start = ((), (), s32[]{:S(2)}) async-start(), calls=%async_computation.4 | async-start | bytes 5242880 | tf_op jit(solution)/shard_map/reduce_scatter | solution.py:15
  79.3 116.5 %all-gather.8.cloned.1.call-start = ((), (), s32[]{:S(2)}) async-start(), calls=%async_computation.5 | async-start | bytes 4718592 | tf_op jit(solution)/shard_map/all_gather | solution.py:14
  158.4 144.6 %reduce-scatter.6.cloned.1.call-start = ((), (), s32[]{:S(2)}) async-start(), calls=%async_computation.6 | async-start | bytes 5242880 | tf_op jit(solution)/shard_map/reduce_scatter | solution.py:15
  226.0 116.4 %all-gather.10.cloned.1.call-start = ((), (), s32[]{:S(2)}) async-start(), calls=%async_computation.7 | async-start | bytes 4718592 | tf_op jit(solution)/shard_map/all_gather | solution.py:14
  305.1 149.8 %reduce-scatter.8.cloned.1.call-start = ((), (), s32[]{:S(2)}) async-start(), calls=%async_computation.8 | async-start | bytes 5242880 | tf_op jit(solution)/shard_map/reduce_scatter | solution.py:15
  377.9 77.0 %copy-start.5 = (f32[1024,256]{1,0:T(8,128)S(1)}, f32[1024,256]{1,0:T(8,128)}, u32[]{:S(2)}) copy-start(f32[1024,256]{1,0:T(8,128)} %reduce-scatter.4.cloned.1.call-done) | copy-start | bytes 3145732
  377.9 159.8 %all-gather.12.cloned.1.call-start = ((), (), s32[]{:S(2)}) async-start(), calls=%async_computation.9 | async-start | bytes 5242880 | tf_op jit(solution)/shard_map/all_gather | solution.py:27
  378.6 240.4 %all-gather.14.cloned.1.call-start = ((), (), s32[]{:S(2)}) async-start(), calls=%async_computation.10 | async-start | bytes 5242880 | tf_op jit(solution)/shard_map/all_gather | solution.py:28
  457.2 245.5 %all-reduce.3.cloned.1.call-start = ((), (), s32[]{:S(2)}) async-start(), calls=%async_computation.11 | async-start | bytes 4718592 | tf_op jit(solution)/shard_map/psum | solution.py:50
  702.6 3.4 copy-start.2
  708.0 1.4 copy-start.4
  848.3 85.0 %copy-start.3 = (f32[768,768]{1,0:T(8,128)S(1)}, f32[768,768]{1,0:T(8,128)}, u32[]{:S(2)}) copy-start(f32[768,768]{1,0:T(8,128)} %fusion.20) | copy-start | bytes 7077892
  930.0 2.8 copy-start.6
  939.7 3.6 copy-start.1
  943.4 2.8 copy-start
Sparse Core Ops, SparseCore 0:
  9.9 39.2 all-gather.5
  79.4 76.7 reduce-scatter.3
  158.8 37.0 all-gather.7
  226.1 76.7 reduce-scatter.5
  305.3 37.0 all-gather.9
  378.0 76.7 reduce-scatter.7
  456.4 81.2 all-gather.11
  539.8 79.2 all-gather.13
  641.1 61.4 all-reduce.2
where the time goes:
time: 965 us; the launch traced here: 959 us
  waiting for transfers between devices  563 us (58%)
  other arithmetic  197 us (20%)
  matrix products  154 us (16%)
  local copies, waits for them, and re-layouts  26.2 us (3%)
  between operations  18.4 us (2%)
    reduce_scatter x3, waiting for transfers between devices, apply_iterate(): lax.psum_scatter(lax.dot_general(flat_iterate, gathered, (((0,), (0,)), (...  230 us
    another operation x22, other arithmetic, body(): lower_factor = jnp.linalg.cholesky(gram)  123 us
    all_gather x3, waiting for transfers between devices, apply_iterate(): gathered = lax.all_gather(vector, 'row', axis=0, tiled=True)  116 us
    dot_general x3, matrix products, apply_iterate(): lax.dot_general(flat_iterate, gathered, (((0,), (0,)), ((), ())), preferr...  95.7 us
    all_gather x1, waiting for transfers between devices, body(): old_gathered = lax.all_gather(old_factor_t, 'col', axis=0, tiled=True)  80.5 us
    all_gather x1, waiting for transfers between devices, body(): panel_gathered = lax.all_gather(panel, 'col', axis=0, tiled=True)  75.6 us
    another operation x3, other arithmetic, body(): jax.scipy.linalg.solve_triangular(lower_factor, identity, lower=True)  62.2 us
    psum x1, waiting for transfers between devices, body(): gram = lax.psum(local_gram, 'row')  59.8 us
  transfers between devices with their start and end apart: 9, of which 9 were waited for; matrix products, arithmetic and copies ran while one was open for 1% of the time, Pallas kernels for 0%

commit v1 on v0

--- a/solution.py
+++ b/solution.py
@@ -47,7 +47,7 @@
         )
         * scale_gram
     )
-    gram = lax.psum(local_gram, "row")
+    gram = jnp.sum(lax.all_gather(local_gram, "row"), axis=0)
     lower_factor = jnp.linalg.cholesky(gram)
     identity = jnp.eye(gram.shape[0], dtype=jnp.float32)
     inverse = jax.scipy.linalg.solve_triangular(lower_factor, identity, lower=True)

time: 965 us -> 1010 us (1.047)
  waiting for transfers between devices: 563 us -> 598 us
    all_gather x0 -> x1, waiting for transfers between devices: none -> 95.5 us  [body(): gram = jnp.sum(lax.all_gather(local_gram, 'row'), axis=0)]
    psum x1 -> x0, waiting for transfers between devices: 59.8 us -> none  [body(): gram = lax.psum(local_gram, 'row')]
where the time goes in v1:
time: 1010 us; the launch traced here: 1000 us
  waiting for transfers between devices  598 us (59%)
  other arithmetic  204 us (20%)
  matrix products  154 us (15%)
  local copies, waits for them, and re-layouts  26.5 us (3%)
  between operations  18.3 us (2%)
    reduce_scatter x3, waiting for transfers between devices, apply_iterate(): lax.psum_scatter(lax.dot_general(flat_iterate, gathered, (((0,), (0,)), (...  229 us
    another operation x22, other arithmetic, body(): lower_factor = jnp.linalg.cholesky(gram)  123 us
    all_gather x3, waiting for transfers between devices, apply_iterate(): gathered = lax.all_gather(vector, 'row', axis=0, tiled=True)  116 us
    dot_general x3, matrix products, apply_iterate(): lax.dot_general(flat_iterate, gathered, (((0,), (0,)), ((), ())), preferr...  95.7 us
    all_gather x1, waiting for transfers between devices, body(): gram = jnp.sum(lax.all_gather(local_gram, 'row'), axis=0)  95.5 us
    all_gather x1, waiting for transfers between devices, body(): old_gathered = lax.all_gather(old_factor_t, 'col', axis=0, tiled=True)  80.4 us
    all_gather x1, waiting for transfers between devices, body(): panel_gathered = lax.all_gather(panel, 'col', axis=0, tiled=True)  75.5 us
    another operation x3, other arithmetic, body(): jax.scipy.linalg.solve_triangular(lower_factor, identity, lower=True)  62.2 us
  transfers between devices with their start and end apart: 9, of which 9 were waited for; matrix products, arithmetic and copies ran while one was open for 1% of the time, Pallas kernels for 0%

profile of v1, /device:TPU:0, one launch (start us, length us, event | category | flops | bytes accessed | tf_op | source)
XLA Modules:
  0.0 1001.6 jit_solution(590455827793759677)
XLA Ops:
  7.2 0.7 all-gather.7.cloned.1.call-update
  7.9 41.3 %all-gather.7.cloned.1.call-done = bf16[8192,256]{1,0:T(8,128)(2,1)} async-done(((bf16[1024,256]{1,0:T(8,128)(2,1)}), bf16[8192,256]{1,0:T(8,128)(2,1)}) %all-gather.7.cloned.1.call-update) | async-done | bytes 4194320 | tf_op jit(solution)/shard_map/all_gather | solution.py:14
  49.2 30.1 %fusion.59 = f32[4096,256]{1,0:T(8,128)} fusion(bf16[8192,4096]{1,0:T(8,128)(2,1)} %bitcast, bf16[8192,256]{1,0:T(8,128)(2,1)} %all-gather.7.cloned.1.call-done), kind=kOutput, calls=%fused_computation.126 | convolution fusion | flops 17179869184 | bytes 75497472 | tf_op jit(solution)/shard_map/dot_general | solution.py:16
  79.4 76.9 %reduce-scatter.4.cloned.1.call-done = f32[1024,256]{1,0:T(8,128)} async-done(((f32[4096,256]{1,0:T(8,128)}), f32[1024,256]{1,0:T(8,128)}) %reduce-scatter.4.cloned.1.call-update) | async-done | bytes 1048592 | tf_op jit(solution)/shard_map/reduce_scatter | solution.py:15
  156.3 2.1 convert_element_type.18
  158.6 37.2 %all-gather.9.cloned.1.call-done = bf16[8192,256]{1,0:T(8,128)(2,1)} async-done(((bf16[1024,256]{1,0:T(8,128)(2,1)}), bf16[8192,256]{1,0:T(8,128)(2,1)}) %all-gather.9.cloned.1.call-update) | async-done | bytes 4194320 | tf_op jit(solution)/shard_map/all_gather | solution.py:14
  195.9 30.1 %convolution_bitcast_fusion.1 = f32[4096,256]{0,1:T(8,128)} fusion(bf16[8192,256]{1,0:T(8,128)(2,1)} %all-gather.9.cloned.1.call-done, bf16[8192,4096]{1,0:T(8,128)(2,1)} %bitcast), kind=kOutput, calls=%fused_computation.3 | convolution fusion | flops 17179869184 | bytes 75497472 | tf_op jit(solution)/shard_map/dot_general | solution.py:16
  226.0 76.9 %reduce-scatter.6.cloned.1.call-done = f32[1024,256]{0,1:T(8,128)} async-done(((f32[4096,256]{0,1:T(8,128)}), f32[1024,256]{0,1:T(8,128)}) %reduce-scatter.6.cloned.1.call-update) | async-done | bytes 1048592 | tf_op jit(solution)/shard_map/reduce_scatter | solution.py:15
  302.9 2.1 convert_element_type.19
  305.1 37.3 %all-gather.11.cloned.1.call-done = bf16[8192,256]{0,1:T(8,128)(2,1)} async-done(((bf16[1024,256]{0,1:T(8,128)(2,1)}), bf16[8192,256]{0,1:T(8,128)(2,1)}) %all-gather.11.cloned.1.call-update) | async-done | bytes 4194320 | tf_op jit(solution)/shard_map/all_gather | solution.py:14
  342.4 35.5 %convolution_bitcast_fusion = f32[4096,256]{1,0:T(8,128)} fusion(bf16[8192,256]{0,1:T(8,128)(2,1)} %all-gather.11.cloned.1.call-done, bf16[8192,4096]{1,0:T(8,128)(2,1)} %bitcast), kind=kOutput, calls=%fused_computation.2 | convolution fusion | flops 17179869184 | bytes 75497472 | tf_op jit(solution)/shard_map/dot_general | solution.py:16
  377.9 0.7 all-gather.13.cloned.1.call-update
  379.1 75.7 %reduce-scatter.8.cloned.1.call-done = f32[1024,256]{1,0:T(8,128)} async-done(((f32[4096,256]{1,0:T(8,128)}), f32[1024,256]{1,0:T(8,128)}) %reduce-scatter.8.cloned.1.call-update) | async-done | bytes 1048592 | tf_op jit(solution)/shard_map/reduce_scatter | solution.py:15
  454.8 2.3 multiply_subtract_fusion
  457.2 80.4 %all-gather.13.cloned.1.call-done = bf16[512,4096]{1,0:T(8,128)(2,1)} async-done(((bf16[128,4096]{1,0:T(8,128)(2,1)}), bf16[512,4096]{1,0:T(8,128)(2,1)}) %all-gather.13.cloned.1.call-update) | async-done | bytes 4194320 | tf_op jit(solution)/shard_map/all_gather | solution.py:27
  537.7 5.9 fusion.60
  543.5 75.5 %all-gather.15.cloned.1.call-done = f32[4096,256]{1,0:T(8,128)} async-done(((f32[1024,256]{1,0:T(8,128)}), f32[4096,256]{1,0:T(8,128)}) %all-gather.15.cloned.1.call-update) | async-done | bytes 4194320 | tf_op jit(solution)/shard_map/all_gather | solution.py:28
  619.1 9.8 fusion.61
  629.1 10.2 %fusion.62 = f32[256,256]{0,1:T(8,128)S(1)} fusion(f32[4096,256]{1,0:T(8,128)} %all-gather.15.cloned.1.call-done), kind=kOutput, calls=%fused_computation.129 | convolution fusion | flops 3221225472 | bytes 4456448 | tf_op jit(solution)/shard_map/dot_general | solution.py:37
  639.8 2.0 copy.14
  641.9 1.6 fusion.20
  643.5 95.5 %all-gather.17.cloned.1.call-done = f32[8,768,768]{2,1,0:T(8,128)} async-done(((f32[1,768,768]{2,1,0:T(8,128)}), f32[8,768,768]{2,1,0:T(8,128)}) %all-gather.17.cloned.1.call-update) | async-done | bytes 18874384 | tf_op jit(solution)/shard_map/all_gather | solution.py:50
  739.0 7.9 reduce_sum.9
  746.8 2.1 copy.15
  749.0 2.0 fusion
  750.9 1.4 copy-done.3
  752.3 11.7 %cholesky.165 = f32[128,128]{1,0:T(8,128)S(1)} custom-call(f32[128,128]{1,0:T(8,128)S(1)} %cholesky.424), custom_call_target="Cholesky" | custom-call | tf_op jit(solution)/shard_map/jit(cholesky)/cholesky | solution.py:51
  764.2 9.8 custom-call.47
  774.1 1.4 constant_dynamic-update-slice_fusion.15
  775.5 1.4 convolution_subtract_fusion.4
  776.9 11.7 %cholesky.188 = f32[128,128]{1,0:T(8,128)S(1)} custom-call(f32[128,128]{1,0:T(8,128)S(1)} %cholesky.428), custom_call_target="Cholesky" | custom-call | tf_op jit(solution)/shard_map/jit(cholesky)/cholesky | solution.py:51
  788.6 10.2 %custom-call.48 = f32[1,128,128]{1,2,0:T(8,128)S(1)} custom-call(f32[1,128,128]{2,1,0:T(8,128)S(1)} %get-tuple-element.42), custom_call_target="InvertDiagBlocksLowerTriangular" | custom-call | tf_op jit(solution)/shard_map/jit(cholesky)/cholesky | solution.py:51
  799.2 1.5 convolution_subtract_fusion.5
  800.7 11.7 %cholesky.354 = f32[128,128]{1,0:T(8,128)S(1)} custom-call(f32[128,128]{1,0:T(8,128)S(1)} %cholesky.433), custom_call_target="Cholesky" | custom-call | tf_op jit(solution)/shard_map/jit(cholesky)/cholesky | solution.py:51
  813.1 9.8 custom-call.49
  823.3 1.6 convolution_subtract_fusion.6
  824.8 11.9 %cholesky.373 = f32[128,128]{1,0:T(8,128)S(1)} custom-call(f32[128,128]{1,0:T(8,128)S(1)} %cholesky.438), custom_call_target="Cholesky" | custom-call | tf_op jit(solution)/shard_map/jit(cholesky)/cholesky | solution.py:51
  836.7 0.7 compare_reduce_fusion.2
  837.4 9.8 custom-call.50
  847.5 1.5 convolution_subtract_fusion.7
  849.0 11.7 %cholesky.392 = f32[128,128]{1,0:T(8,128)S(1)} custom-call(f32[128,128]{1,0:T(8,128)S(1)} %cholesky.443), custom_call_target="Cholesky" | custom-call | tf_op jit(solution)/shard_map/jit(cholesky)/cholesky | solution.py:51
  860.7 0.7 compare_reduce_fusion.1
  861.5 9.8 custom-call.51
  871.5 1.3 convolution_subtract_fusion.8
  872.8 11.7 %cholesky.410 = f32[128,128]{1,0:T(8,128)S(1)} custom-call(f32[128,128]{1,0:T(8,128)S(1)} %convolution_subtract_fusion.8), custom_call_target="Cholesky" | custom-call | tf_op jit(solution)/shard_map/jit(cholesky)/cholesky | solution.py:51
  884.5 0.7 compare_reduce_fusion
  885.2 0.6 compare_reduce_fusion.4
  889.6 1.6 select_select_fusion
  891.2 20.7 %while.1 = (s32[]{:T(128)}, f32[768,768]{1,0:T(8,128)}, s32[6,2]{0,1:T(2,128)S(1)}, f32[6,128,128]{2,1,0:T(8,128)}, s32[]{:T(128)}) while((s32[]{:T(128)}, f32[768,768]{1,0:T(8,128)}, s32[6,2]{0,1:T(2,128)S(1)}, f32[6,128,128]{2,1,0:T(8,128)}, s32[]{:T(128)}) %tuple.44), condition=%wide.while_cond, body=%wide.while_body.sunk | while | flops 2 | bytes 132705 | solution.py:53
  891.8 2.9 bitcast_dynamic-update-slice_fusion.2
  895.3 2.8 bitcast_dynamic-update-slice_fusion.2
  898.7 2.8 bitcast_dynamic-update-slice_fusion.2
  902.2 2.8 bitcast_dynamic-update-slice_fusion.2
  905.6 2.8 bitcast_dynamic-update-slice_fusion.2
  909.1 2.8 bitcast_dynamic-update-slice_fusion.2
  911.8 60.6 %custom-call.52 = f32[6,128,128]{1,2,0:T(8,128)} custom-call(f32[6,128,128]{2,1,0:T(8,128)} %get-tuple-element.9), custom_call_target="InvertDiagBlocksLowerTriangular" | custom-call | tf_op jit(solution)/shard_map/jit(_solve_triangular)/triangular_solve | solution.py:53
  972.4 1.3 constant_dynamic-update-slice_fusion.4
  973.7 1.5 convolution_subtract_fusion.2
  975.8 1.5 convolution_subtract_fusion.3
  977.8 1.8 convolution_subtract_fusion.1
  980.2 2.0 fusion.9
  982.7 2.6 convolution_subtract_fusion
  985.8 2.8 fusion.24
  988.6 6.2 convolution_add_fusion
  (69 shorter events, 10.4 us)
Async XLA Ops:
  7.2 42.0 %all-gather.7.cloned.1.call-start = ((), (), s32[]{:S(2)}) async-start(), calls=%async_computation.3 | async-start | bytes 4718592 | tf_op jit(solution)/shard_map/all_gather | solution.py:14
  7.9 148.4 %reduce-scatter.4.cloned.1.call-start = ((), (), s32[]{:S(2)}) async-start(), calls=%async_computation.4 | async-start | bytes 5242880 | tf_op jit(solution)/shard_map/reduce_scatter | solution.py:15
  79.3 116.5 %all-gather.9.cloned.1.call-start = ((), (), s32[]{:S(2)}) async-start(), calls=%async_computation.5 | async-start | bytes 4718592 | tf_op jit(solution)/shard_map/all_gather | solution.py:14
  158.4 144.6 %reduce-scatter.6.cloned.1.call-start = ((), (), s32[]{:S(2)}) async-start(), calls=%async_computation.6 | async-start | bytes 5242880 | tf_op jit(solution)/shard_map/reduce_scatter | solution.py:15
  226.0 116.4 %all-gather.11.cloned.1.call-start = ((), (), s32[]{:S(2)}) async-start(), calls=%async_computation.7 | async-start | bytes 4718592 | tf_op jit(solution)/shard_map/all_gather | solution.py:14
  305.1 149.8 %reduce-scatter.8.cloned.1.call-start = ((), (), s32[]{:S(2)}) async-start(), calls=%async_computation.8 | async-start | bytes 5242880 | tf_op jit(solution)/shard_map/reduce_scatter | solution.py:15
  377.9 77.0 %copy-start.4 = (f32[1024,256]{1,0:T(8,128)S(1)}, f32[1024,256]{1,0:T(8,128)}, u32[]{:S(2)}) copy-start(f32[1024,256]{1,0:T(8,128)} %reduce-scatter.4.cloned.1.call-done) | copy-start | bytes 3145732
  377.9 159.8 %all-gather.13.cloned.1.call-start = ((), (), s32[]{:S(2)}) async-start(), calls=%async_computation.9 | async-start | bytes 5242880 | tf_op jit(solution)/shard_map/all_gather | solution.py:27
  378.6 240.4 %all-gather.15.cloned.1.call-start = ((), (), s32[]{:S(2)}) async-start(), calls=%async_computation.10 | async-start | bytes 5242880 | tf_op jit(solution)/shard_map/all_gather | solution.py:28
  457.2 281.8 %all-gather.17.cloned.1.call-start = ((), (), s32[]{:S(2)}) async-start(), calls=%async_computation.11 | async-start | bytes 21233664 | tf_op jit(solution)/shard_map/all_gather | solution.py:50
  750.9 1.4 copy-start.3
  891.2 84.6 %copy-start.2 = (f32[768,768]{1,0:T(8,128)S(1)}, f32[768,768]{1,0:T(8,128)}, u32[]{:S(2)}) copy-start(f32[768,768]{1,0:T(8,128)} %fusion.20) | copy-start | bytes 7077892
  972.4 2.8 copy-start.5
  982.1 3.6 copy-start.1
  985.8 2.8 copy-start
Sparse Core Ops, SparseCore 0:
  9.9 39.2 all-gather.6
  79.5 76.7 reduce-scatter.3
  158.8 37.0 all-gather.8
  226.1 76.7 reduce-scatter.5
  305.3 37.0 all-gather.10
  378.0 76.7 reduce-scatter.7
  456.4 81.2 all-gather.12
  539.8 79.2 all-gather.14
  641.9 97.0 all-gather.16
